TPU v7x, 128 devices: a whole 4x4x4 slice. The times are simulated.
128 devices in a mesh: row: 8 (over x_lo, z), col: 16 (over y, x_hi, core).
Axes of the slice: x: 4 (x_hi: 2, x_lo: 2; x = x_hi * 2 + x_lo), y: 4, z: 4, core: 2. Of those that a mesh axis runs over, the one named last changes fastest.
Arguments:
- amplitudes: bfloat16 [32, 32, 12, 4096], P('row', 'col'), may hold values from -6 to 6
- integrals: bfloat16 [32, 32, 47, 4096], P('row', 'col'), may hold values from -0.125 to 0.125
- pair_lists: int32 [8, 12, 2], replicated, may hold values from 0 to 46, as said below
- tile_counts: int32 [8], replicated, may hold values from 1 to 12, as said below
Outputs:
- symmetric: float32 [32, 32, 12, 4096], P('row', 'col')
Inputs may be any that keep to these rules, and one draw needn't show every extreme that they name: `pair_lists`: each grid row lists 12 distinct ordered pairs of different tiles. `tile_counts`: the largest count equals 12.
All inputs are finite; a program needn't handle non-finite values.
Results may differ from a plain program's by a relative error of at most 0.0029.
Values may be sent and summed in bfloat16 or wider, within the bound.
A program may use at most 128 MiB of HBM per device.

v0:
```python
import jax
import jax.numpy as jnp
from jax import lax
from jax.sharding import PartitionSpec as P

TILE = 64


def spread(block, axis, owner):
    block = jnp.where(lax.axis_index(axis) == owner, block, jnp.zeros_like(block))
    return lax.psum(block, axis)


def on_device(amplitudes, integrals, pair_lists, tile_counts):
    occ_row, occ_col, slot_count, square = amplitudes.shape
    tile_width = TILE
    row_devices = lax.axis_size("row")
    col_devices = lax.axis_size("col")
    col_ratio = col_devices // row_devices
    my_row = lax.axis_index("row")
    my_col = lax.axis_index("col")
    partner_row = my_col // col_ratio
    tile_first = pair_lists[:, :, 0]
    tile_second = pair_lists[:, :, 1]
    packed = jnp.take(integrals, tile_second.reshape(-1), axis=2)
    packed = packed.reshape(occ_row, occ_col, row_devices, slot_count, square)
    received = lax.all_to_all(packed, "row", split_axis=2, concat_axis=0, tiled=True)
    received = received.reshape(occ_row * row_devices, occ_col, slot_count, square)
    piece = lax.all_gather(amplitudes, "col", axis=1, tiled=True)
    piece_count = piece.shape[1]
    left_tiles = piece.reshape(occ_row, piece_count, slot_count, tile_width, tile_width)
    right_tiles = received.reshape(piece_count, occ_col, slot_count, tile_width, tile_width)
    cycle_sum = jnp.einsum(
        "iksac,kjscb->ijsab", left_tiles, right_tiles, preferred_element_type=jnp.float32
    )
    my_count = lax.dynamic_index_in_dim(tile_counts, my_row, 0, keepdims=False)
    live_slots = (jnp.arange(slot_count, dtype=jnp.int32) < my_count).astype(jnp.float32)
    cycle_value = (cycle_sum * live_slots[None, None, :, None, None]).astype(jnp.bfloat16)
    cycle = cycle_value.reshape(occ_row, occ_col, slot_count, square)
    residual_strip = lax.all_gather(cycle, "col", axis=1, tiled=True)
    mirror_part = lax.dynamic_slice_in_dim(residual_strip, my_col % col_ratio * occ_col, occ_col, 0)
    mirror_whole = spread(mirror_part, "row", partner_row)
    mirror_block = lax.dynamic_slice_in_dim(mirror_whole, my_row * occ_row, occ_row, 1)
    mirror_block = mirror_block.reshape(occ_col, occ_row, slot_count, tile_width, tile_width)
    mine_first = lax.dynamic_index_in_dim(tile_first, my_row, 0, keepdims=False)
    mine_second = lax.dynamic_index_in_dim(tile_second, my_row, 0, keepdims=False)
    their_first = lax.dynamic_index_in_dim(tile_first, partner_row, 0, keepdims=False)
    their_second = lax.dynamic_index_in_dim(tile_second, partner_row, 0, keepdims=False)
    pair_match = (
        (mine_first[:, None] == their_second[None, :])
        & (mine_second[:, None] == their_first[None, :])
    ).astype(jnp.bfloat16)
    crossed = jnp.einsum(
        "st,jitba->ijsab", pair_match, mirror_block, preferred_element_type=jnp.float32
    )
    own_part = cycle_value.astype(jnp.float32)
    symmetric = (own_part + crossed) * live_slots[None, None, :, None, None]
    return symmetric.reshape(occ_row, occ_col, slot_count, square)


def solution(mesh):
    return jax.shard_map(
        on_device,
        mesh=mesh,
        in_specs=(P("row", "col", None, None), P("row", "col", None, None), P(), P()),
        out_specs=P("row", "col", None, None),
        check_vma=False,
    )
```

profile of v0, /device:TPU:1, one launch (start us, length us, event | category | flops | bytes accessed | tf_op | source)
XLA Modules:
  0.0 507.0 jit_solution(17754718859662884650)
XLA Ops:
  6.5 2.8 copy.18
  9.3 0.8 fusion.29
  10.2 15.2 %gather_fusion = bf16[96,4,2,4096]{3,2,1,0:T(2,128)(2,1)} fusion(bf16[4,2,47,4096]{3,1,2,0:T(2,128)(2,1)S(1)} %copy-done, s32[1024]{0:T(1024)S(1)} %pad_clamp_fusion), kind=kCustom, calls=%fused_computation | custom fusion | bytes 12583296 | tf_op jit(solution)/shard_map/jit(_take)/gather | solution.py:25
  25.5 8.5 %broadcast_select_fusion.1 = bf16[4,2,8,12,4096]{4,1,3,0,2:T(2,128)(2,1)} fusion(pred[8,12]{1,0:T(8,128)(4,1)S(1)} %compare_and_fusion, bf16[4,2,8,12,4096]{4,1,0,3,2:T(2,128)(2,1)} %bitcast.67), kind=kLoop, calls=%fused_computation.5 | loop fusion | flops 3145728 | bytes 12583008 | tf_op jit(solution)/shard_map/jit(_take)/select_n | solution.py:25
  33.9 6.9 %all-to-all-start = ((bf16[4,2,8,12,4096]{4,1,3,0,2:T(2,128)(2,1)}), bf16[4,2,8,12,4096]{4,1,3,0,2:T(2,128)(2,1)}, u32[]{:S(2)}, u32[]{:S(2)}) async-start(bf16[4,2,8,12,4096]{4,1,3,0,2:T(2,128)(2,1)} %broadcast_select_fusion.1), calls=%async_computation | async-start | bytes 12582912 | tf_op jit(solution)/shard_map/all_to_all | solution.py:27
  41.1 0.6 dynamic_slice.23
  41.7 0.6 compare_convert_fusion
  42.3 101.4 %all-to-all-done = bf16[4,2,8,12,4096]{4,1,3,0,2:T(2,128)(2,1)} async-done(((bf16[4,2,8,12,4096]{4,1,3,0,2:T(2,128)(2,1)}), bf16[4,2,8,12,4096]{4,1,3,0,2:T(2,128)(2,1)}, u32[]{:S(2)}, u32[]{:S(2)}) %all-to-all-start) | async-done | bytes 6291488 | tf_op jit(solution)/shard_map/all_to_all | solution.py:27
  143.6 20.6 %reshape_reshape.3 = bf16[32,2,12,64,64]{4,3,1,2,0:T(8,128)(2,1)} reshape(bf16[8,4,2,1,12,4096]{5,2,4,1,0,3:T(2,128)(2,1)} %bitcast.5) | data formatting | bytes 12582912 | tf_op jit(solution)/shard_map/reshape;reshape | solution.py:32
  164.2 14.4 %copy.19 = bf16[4,32,12,4096]{3,1,0,2:T(8,128)(2,1)} copy(bf16[4,32,12,4096]{3,0,2,1:T(4,128)(2,1)} %all-gather.3.cloned.1.call-done) | data formatting | bytes 25165824 | tf_op jit(solution)/shard_map/all_gather | solution.py:29
  178.6 34.4 %reshape.81 = bf16[4,32,12,64,64,1]{4,3,1,0,2,5:T(8,128)(2,1)} reshape(bf16[4,32,12,4096]{3,1,0,2:T(8,128)(2,1)} %copy.19) | data formatting | bytes 25165824 | tf_op jit(solution)/shard_map/reshape | solution.py:31
  213.0 19.0 %fusion.11 = bf16[4,2,12,64,64]{3,4,0,1,2:T(8,128)(2,1)S(1)} fusion(f32[12]{0:T(128)S(1)} %compare_convert_fusion, bf16[4,32,12,64,64,1]{4,3,1,0,2,5:T(8,128)(2,1)} %reshape.81, bf16[32,2,12,64,64]{4,3,1,2,0:T(8,128)(2,1)} %reshape_reshape.3), kind=kOutput, calls=%fused_computation.12 | convolution fusion | flops 1611399168 | bytes 19660848 | tf_op jit(solution)/shard_map/iksac,kjscb->ijsab/dot_general | solution.py:33
  232.1 1.8 copy.33
  233.8 3.7 reshape.85
  237.5 0.3 all-reduce.2.cloned.1.call-start
  237.8 93.1 %all-gather.5.cloned.1.call-done = bf16[4,32,12,4096]{3,0,2,1:T(4,128)(2,1)} async-done(((bf16[4,2,12,4096]{3,0,2,1:T(4,128)(2,1)}), bf16[4,32,12,4096]{3,0,2,1:T(4,128)(2,1)}) %all-gather.5.cloned.1.call-update) | async-done | bytes 12582928 | tf_op jit(solution)/shard_map/all_gather | solution.py:40
  330.9 10.8 %broadcast_select_fusion = bf16[2,32,12,4096]{3,0,2,1:T(2,128)(2,1)} fusion(pred[]{:T(512)S(6)} %eq.39, bf16[4,32,12,4096]{3,0,2,1:T(4,128)(2,1)} %all-gather.5.cloned.1.call-done, s32[]{:T(128)S(6)} %select_n.65), kind=kLoop, calls=%fused_computation.4 | loop fusion | flops 3145728 | bytes 12582917 | tf_op jit(solution)/shard_map/jit(_where)/select_n | solution.py:10
  341.7 142.5 %all-reduce.2.cloned.1.call-done = bf16[2,32,12,4096]{3,0,2,1:T(2,128)(2,1)} async-done(((bf16[2,32,12,4096]{3,0,2,1:T(2,128)(2,1)}), bf16[2,32,12,4096]{3,0,2,1:T(2,128)(2,1)}) %all-reduce.2.cloned.1.call-update) | async-done | bytes 6291472 | tf_op jit(solution)/shard_map/psum | solution.py:11
  484.3 2.0 constant_dynamic-slice_fusion.4
  486.3 1.0 reshape.86
  487.3 1.1 fusion.5
  488.4 4.3 fusion.3
  492.7 3.6 copy.26
  496.3 4.2 reshape.71
  (20 shorter events, 0.4 us)
Async XLA Ops:
  6.5 3.7 copy-start
  6.5 157.7 %all-gather.3.cloned.1.call-start = ((), (), s32[]{:S(2)}) async-start(), calls=%async_computation.1 | async-start | bytes 13369344 | tf_op jit(solution)/shard_map/all_gather | solution.py:29
  33.9 7.2 %copy-start.3 = (s32[8]{0:T(128)S(1)}, s32[8]{0:T(128)}, u32[]{:S(2)}) copy-start(s32[8]{0:T(128)} %param.7) | copy-start | bytes 100
  33.9 109.7 %all-to-all-start = ((bf16[4,2,8,12,4096]{4,1,3,0,2:T(2,128)(2,1)}), bf16[4,2,8,12,4096]{4,1,3,0,2:T(2,128)(2,1)}, u32[]{:S(2)}, u32[]{:S(2)}) async-start(bf16[4,2,8,12,4096]{4,1,3,0,2:T(2,128)(2,1)} %broadcast_select_fusion.1), calls=%async_computation | async-start | bytes 12582912 | tf_op jit(solution)/shard_map/all_to_all | solution.py:27
  40.9 290.0 %all-gather.5.cloned.1.call-start = ((), (), s32[]{:S(2)}) async-start(), calls=%async_computation.2 | async-start | bytes 13369344 | tf_op jit(solution)/shard_map/all_gather | solution.py:40
  232.0 109.6 %copy-start.2 = (bf16[4,2,12,64,64]{3,4,0,1,2:T(8,128)(2,1)}, bf16[4,2,12,64,64]{3,4,0,1,2:T(8,128)(2,1)S(1)}, u32[]{:S(2)}) copy-start(bf16[4,2,12,64,64]{3,4,0,1,2:T(8,128)(2,1)S(1)} %fusion.11) | copy-start | bytes 2359300
  237.5 246.7 %all-reduce.2.cloned.1.call-start = ((), (), s32[]{:S(2)}) async-start(), calls=%async_computation.3 | async-start | bytes 12582912 | tf_op jit(solution)/shard_map/psum | solution.py:11
  488.4 12.0 %copy-start.1 = (bf16[4,2,47,4096]{3,1,2,0:T(2,128)(2,1)S(1)}, bf16[4,2,47,4096]{3,1,2,0:T(2,128)(2,1)}, u32[]{:S(2)}) copy-start(bf16[4,2,47,4096]{3,1,2,0:T(2,128)(2,1)} %param.5) | copy-start | bytes 9240580
Sparse Core Ops, SparseCore 0:
  9.8 128.3 all-gather.2
  237.6 93.2 all-gather.4
  341.8 142.4 all-reduce.1
where the time goes:
time: 509 us; the launch traced here: 507 us
  waiting for transfers between devices  337 us (66%)
  local copies, waits for them, and re-layouts  105 us (21%)
  other arithmetic  24.1 us (5%)
  matrix products  20.1 us (4%)
  between operations  13.2 us (3%)
  starting transfers between devices  7.4 us (1%)
    psum x1, waiting for transfers between devices, spread(): return lax.psum(block, axis)  143 us
    all_to_all x1, waiting for transfers between devices, on_device(): lax.all_to_all(packed, 'row', split_axis=2, concat_axis=0, tiled=True)  101 us
    all_gather x1, waiting for transfers between devices, on_device(): residual_strip = lax.all_gather(cycle, 'col', axis=1, tiled=True)  93.1 us
    reshape x1, local copies, waits for them, and re-layouts, on_device(): piece.reshape(occ_row, piece_count, slot_count, tile_width, tile_width)  34.4 us
    another operation x1, local copies, waits for them, and re-layouts, on_device(): received.reshape(piece_count, occ_col, slot_count, tile_width, tile_width)  20.6 us
    dot_general x1, matrix products, on_device(): jnp.einsum('iksac,kjscb->ijsab', left_tiles, right_tiles, preferred_eleme...  19 us
    gather x1, local copies, waits for them, and re-layouts, on_device(): packed = jnp.take(integrals, tile_second.reshape(-1), axis=2)  15.2 us
    all_gather x1, local copies, waits for them, and re-layouts, on_device(): piece = lax.all_gather(amplitudes, 'col', axis=1, tiled=True)  14.4 us
  transfers between devices with their start and end apart: 4, of which 3 were waited for; matrix products, arithmetic and copies ran while one was open for 9% of the time, Pallas kernels for 0%

commit v1 on v0

--- a/solution.py
+++ b/solution.py
@@ -8,7 +8,7 @@
 
 def spread(block, axis, owner):
     block = jnp.where(lax.axis_index(axis) == owner, block, jnp.zeros_like(block))
-    return lax.psum(block, axis)
+    return jnp.sum(lax.all_gather(block, axis), axis=0)
 
 
 def on_device(amplitudes, integrals, pair_lists, tile_counts):

time: 509 us -> 875 us (1.72)
  waiting for transfers between devices: 337 us -> 678 us
  other arithmetic: 24.1 us -> 43.1 us
    all_gather x0 -> x1, waiting for transfers between devices: none -> 483 us  [spread(): return jnp.sum(lax.all_gather(block, axis), axis=0)]
    psum x1 -> x0, waiting for transfers between devices: 143 us -> none  [spread(): return lax.psum(block, axis)]
    reduce_sum x0 -> x1, other arithmetic: none -> 20 us  [spread(): return jnp.sum(lax.all_gather(block, axis), axis=0)]
  transfers between devices with their start and end apart: 4 -> 4, of which waited for: 3 -> 3; matrix products, arithmetic and copies ran while one was open for 9% -> 5% of each run, Pallas kernels for 0% -> 0%
where the time goes in v1:
time: 875 us; the launch traced here: 873 us
  waiting for transfers between devices  678 us (77%)
  local copies, waits for them, and re-layouts  112 us (13%)
  other arithmetic  43.1 us (5%)
  matrix products  20.1 us (2%)
  between operations  13.3 us (2%)
    all_gather x1, waiting for transfers between devices, spread(): return jnp.sum(lax.all_gather(block, axis), axis=0)  483 us
    all_to_all x1, waiting for transfers between devices, on_device(): lax.all_to_all(packed, 'row', split_axis=2, concat_axis=0, tiled=True)  101 us
    all_gather x1, waiting for transfers between devices, on_device(): residual_strip = lax.all_gather(cycle, 'col', axis=1, tiled=True)  93.3 us
    reshape x1, local copies, waits for them, and re-layouts, on_device(): piece.reshape(occ_row, piece_count, slot_count, tile_width, tile_width)  34.4 us
    another operation x1, local copies, waits for them, and re-layouts, on_device(): received.reshape(piece_count, occ_col, slot_count, tile_width, tile_width)  20.6 us
    reduce_sum x1, other arithmetic, spread(): return jnp.sum(lax.all_gather(block, axis), axis=0)  20 us
    dot_general x1, matrix products, on_device(): jnp.einsum('iksac,kjscb->ijsab', left_tiles, right_tiles, preferred_eleme...  19 us
  transfers between devices with their start and end apart: 4, of which 3 were waited for; matrix products, arithmetic and copies ran while one was open for 5% of the time, Pallas kernels for 0%

profile of v1, /device:TPU:1, one launch (start us, length us, event | category | flops | bytes accessed | tf_op | source)
XLA Modules:
  0.0 873.3 jit_solution(3558723820480005308)
XLA Ops:
  6.5 2.8 copy.18
  9.3 0.8 fusion.29
  10.2 15.2 %gather_fusion = bf16[96,4,2,4096]{3,2,1,0:T(2,128)(2,1)} fusion(bf16[4,2,47,4096]{3,1,2,0:T(2,128)(2,1)S(1)} %copy-done, s32[1024]{0:T(1024)S(1)} %pad_clamp_fusion), kind=kCustom, calls=%fused_computation | custom fusion | bytes 12583296 | tf_op jit(solution)/shard_map/jit(_take)/gather | solution.py:25
  25.5 8.5 broadcast_select_fusion.1
  33.9 6.9 all-to-all-start
  41.1 0.6 dynamic_slice.23
  42.3 101.4 %all-to-all-done = bf16[4,2,8,12,4096]{4,1,3,0,2:T(2,128)(2,1)} async-done(((bf16[4,2,8,12,4096]{4,1,3,0,2:T(2,128)(2,1)}), bf16[4,2,8,12,4096]{4,1,3,0,2:T(2,128)(2,1)}, u32[]{:S(2)}, u32[]{:S(2)}) %all-to-all-start) | async-done | bytes 6291488 | tf_op jit(solution)/shard_map/all_to_all | solution.py:27
  143.6 20.6 %reshape_reshape.3 = bf16[32,2,12,64,64]{4,3,1,2,0:T(8,128)(2,1)} reshape(bf16[8,4,2,1,12,4096]{5,2,4,1,0,3:T(2,128)(2,1)} %bitcast.5) | data formatting | bytes 12582912 | tf_op jit(solution)/shard_map/reshape;reshape | solution.py:32
  164.2 14.4 %copy.19 = bf16[4,32,12,4096]{3,1,0,2:T(8,128)(2,1)} copy(bf16[4,32,12,4096]{3,0,2,1:T(4,128)(2,1)} %all-gather.5.cloned.1.call-done) | data formatting | bytes 25165824 | tf_op jit(solution)/shard_map/all_gather | solution.py:29
  178.6 34.4 %reshape.82 = bf16[4,32,12,64,64,1]{4,3,1,0,2,5:T(8,128)(2,1)} reshape(bf16[4,32,12,4096]{3,1,0,2:T(8,128)(2,1)} %copy.19) | data formatting | bytes 25165824 | tf_op jit(solution)/shard_map/reshape | solution.py:31
  213.0 19.0 %fusion.11 = bf16[4,2,12,64,64]{3,4,0,1,2:T(8,128)(2,1)S(1)} fusion(f32[12]{0:T(128)S(1)} %compare_convert_fusion, bf16[4,32,12,64,64,1]{4,3,1,0,2,5:T(8,128)(2,1)} %reshape.82, bf16[32,2,12,64,64]{4,3,1,2,0:T(8,128)(2,1)} %reshape_reshape.3), kind=kOutput, calls=%fused_computation.12 | convolution fusion | flops 1611399168 | bytes 19660848 | tf_op jit(solution)/shard_map/iksac,kjscb->ijsab/dot_general | solution.py:33
  232.1 1.6 copy.33
  233.7 3.7 reshape.86
  237.5 93.3 %all-gather.7.cloned.1.call-done = bf16[4,32,12,4096]{3,0,2,1:T(4,128)(2,1)} async-done(((bf16[4,2,12,4096]{3,0,2,1:T(4,128)(2,1)}), bf16[4,32,12,4096]{3,0,2,1:T(4,128)(2,1)}) %all-gather.7.cloned.1.call-update) | async-done | bytes 12582928 | tf_op jit(solution)/shard_map/all_gather | solution.py:40
  330.8 9.8 %broadcast_select_fusion = bf16[2,32,12,4096]{3,0,2,1:T(2,128)(2,1)S(1)} fusion(pred[]{:T(512)S(6)} %eq.39, bf16[4,32,12,4096]{3,0,2,1:T(4,128)(2,1)} %all-gather.7.cloned.1.call-done, s32[]{:T(128)S(6)} %select_n.65), kind=kLoop, calls=%fused_computation.4 | loop fusion | flops 3145728 | bytes 12582917 | tf_op jit(solution)/shard_map/jit(_where)/select_n | solution.py:10
  340.6 7.1 copy.23
  347.7 482.8 %all-gather.9.cloned.1.call-done = bf16[16,32,12,4096]{3,1,2,0:T(8,128)(2,1)} async-done(((bf16[2,32,12,4096]{3,1,2,0:T(8,128)(2,1)}), bf16[16,32,12,4096]{3,1,2,0:T(8,128)(2,1)}) %all-gather.9.cloned.1.call-update) | async-done | bytes 50331664 | tf_op jit(solution)/shard_map/all_gather | solution.py:11
  830.5 20.0 %reduce_sum.12 = bf16[2,32,12,4096]{3,1,2,0:T(8,128)(2,1)} reduce(bf16[8,2,32,12,4096]{4,2,3,1,0:T(8,128)(2,1)} %bitcast.68, bf16[]{:T(256)} %constant.74.clone.1), dimensions={0}, to_apply=%region_0.1 | reduce | flops 22020096 | bytes 56623104 | tf_op jit(solution)/shard_map/reduce_sum | solution.py:11
  850.5 1.9 constant_dynamic-slice_fusion.4
  852.4 1.3 reshape.70
  853.7 1.1 fusion.5
  854.8 4.3 fusion.3
  859.1 3.6 copy.26
  862.6 4.2 reshape.71
  (22 shorter events, 1.0 us)
Async XLA Ops:
  6.5 3.7 copy-start
  6.5 157.7 %all-gather.5.cloned.1.call-start = ((), (), s32[]{:S(2)}) async-start(), calls=%async_computation.1 | async-start | bytes 13369344 | tf_op jit(solution)/shard_map/all_gather | solution.py:29
  33.9 7.2 copy-start.3
  33.9 109.7 %all-to-all-start = ((bf16[4,2,8,12,4096]{4,1,3,0,2:T(2,128)(2,1)}), bf16[4,2,8,12,4096]{4,1,3,0,2:T(2,128)(2,1)}, u32[]{:S(2)}, u32[]{:S(2)}) async-start(bf16[4,2,8,12,4096]{4,1,3,0,2:T(2,128)(2,1)} %broadcast_select_fusion.1), calls=%async_computation | async-start | bytes 12582912 | tf_op jit(solution)/shard_map/all_to_all | solution.py:27
  40.9 289.9 %all-gather.7.cloned.1.call-start = ((), (), s32[]{:S(2)}) async-start(), calls=%async_computation.2 | async-start | bytes 13369344 | tf_op jit(solution)/shard_map/all_gather | solution.py:40
  232.0 108.5 %copy-start.2 = (bf16[4,2,12,64,64]{3,4,0,1,2:T(8,128)(2,1)}, bf16[4,2,12,64,64]{3,4,0,1,2:T(8,128)(2,1)S(1)}, u32[]{:S(2)}) copy-start(bf16[4,2,12,64,64]{3,4,0,1,2:T(8,128)(2,1)S(1)} %fusion.11) | copy-start | bytes 2359300
  237.4 593.2 %all-gather.9.cloned.1.call-start = ((), (), s32[]{:S(2)}) async-start(), calls=%async_computation.3 | async-start | bytes 56623104 | tf_op jit(solution)/shard_map/all_gather | solution.py:11
  854.8 12.0 %copy-start.1 = (bf16[4,2,47,4096]{3,1,2,0:T(2,128)(2,1)S(1)}, bf16[4,2,47,4096]{3,1,2,0:T(2,128)(2,1)}, u32[]{:S(2)}) copy-start(bf16[4,2,47,4096]{3,1,2,0:T(2,128)(2,1)} %param.5) | copy-start | bytes 9240580
Sparse Core Ops, SparseCore 0:
  9.8 128.3 all-gather.4
  237.5 93.2 all-gather.6
  347.8 482.6 all-gather.8
